TPU v7x, 128 devices: a whole 4x4x4 slice. The times are simulated.
128 devices in a mesh: var: 4 (over z_hi, core), space: 32 (over z_lo, x, y).
Axes of the slice: x: 4, y: 4, z: 4 (z_hi: 2, z_lo: 2; z = z_hi * 2 + z_lo), core: 2. Of those that a mesh axis runs over, the one named last changes fastest.
Arguments:
- fields: bfloat16 [8, 1024, 131072], P('var', None, 'space'), may hold values from -6 to 6
- eigenfunctions: bfloat16 [8, 64, 131072], P('var', None, 'space'), may hold values from -0.015625 to 0.015625
- start: float32 [512, 128], replicated, may hold values from -6 to 6
- grid_count: int32 [8], replicated, may hold values from 65536 to 131072
Outputs:
- loadings: bfloat16 [8, 128, 131072], P('var', None, 'space')
- component_scores: float32 [1024, 128], replicated
- explained: float32 [8, 1024], P('var')
Inputs may be any that keep to these rules, and one draw needn't show every extreme that they name: The grid of variable v is its points 0 to grid_count[v] - 1.
All inputs are finite; a program needn't handle non-finite values.
Results may differ from a plain program's by a relative error of at most 0.005.
Values sent between devices are 32-bit elements; how exact they have to be, the bound alone decides.
No kernel may reach another device: no remote copies, remote signals or barrier semaphores. Data moves between devices by JAX's collectives and lax.ppermute only.
A program may use at most 64 MiB of HBM per device.

v0:
```python
import jax
import jax.numpy as jnp
from jax import lax
from jax.experimental import pallas as pl
from jax.experimental.pallas import tpu as pltpu
from jax.sharding import Mesh, PartitionSpec as P

M = 64
K = 128
SWEEPS = 2
HIGHEST = lax.Precision.HIGHEST
F32 = jnp.float32
BF16 = jnp.bfloat16
STEP = 512


def dot(left, right, lc, rc, precision=None):
    return lax.dot_general(
        left, right, (((lc,), (rc,)), ((), ())), precision=precision, preferred_element_type=F32
    )


def masked_part(e, first, count):
    columns = first + lax.broadcasted_iota(jnp.int32, e.shape, 1)
    return jnp.where(columns < count, e.astype(F32), 0.0).astype(BF16)


def local_counts(count_ref, points):
    var = lax.axis_index("zh") * lax.axis_size("core") + lax.axis_index("core")
    first = lax.axis_index("space") * points
    return count_ref[2 * var] - first, count_ref[2 * var + 1] - first


def project_kernel(points, peers, count_ref, f_ref, e_ref, out_ref, acc_ref):
    step = pl.program_id(0)
    count0, count1 = local_counts(count_ref, points)
    samples = f_ref.shape[1]
    width = f_ref.shape[2]
    e0 = masked_part(e_ref[0], step * width, count0)
    e1 = masked_part(e_ref[1], step * width, count1)
    none = jnp.zeros_like(e0)
    right0 = jnp.concatenate([e0, none], axis=0)
    right1 = jnp.concatenate([none, e1], axis=0)

    @pl.when(step == 0)
    def _():
        acc_ref[...] = jnp.zeros_like(acc_ref)

    acc_ref[:samples] += dot(f_ref[0], right0, 1, 1) + dot(f_ref[1], right1, 1, 1)
    acc_ref[samples:] += dot(e0, right0, 1, 1) + dot(e1, right1, 1, 1)

    @pl.when(step == pl.num_programs(0) - 1)
    def _():
        own, extra = samples // peers, M // peers
        size = own + extra
        for peer in range(peers):
            out_ref[peer * size : peer * size + own] = acc_ref[peer * own : (peer + 1) * own]
            out_ref[peer * size + own : (peer + 1) * size] = acc_ref[
                samples + peer * extra : samples + (peer + 1) * extra
            ]


def project(fields, eigenfunctions, grid_count, peers):
    _, samples, points = fields.shape
    rows = samples + M
    return pl.pallas_call(
        lambda *refs: project_kernel(points, peers, *refs),
        name="project",
        out_shape=jax.ShapeDtypeStruct((rows, 2 * M), F32),
        grid_spec=pltpu.PrefetchScalarGridSpec(
            num_scalar_prefetch=1,
            grid=(points // STEP,),
            in_specs=[
                pl.BlockSpec((2, samples, STEP), lambda i, c: (0, 0, i)),
                pl.BlockSpec((2, M, STEP), lambda i, c: (0, 0, i)),
            ],
            out_specs=pl.BlockSpec((rows, 2 * M), lambda i, c: (0, 0)),
            scratch_shapes=[pltpu.VMEM((rows, 2 * M), F32)],
        ),
        compiler_params=pltpu.CompilerParams(
            dimension_semantics=("arbitrary",), vmem_limit_bytes=32 << 20
        ),
    )(grid_count, fields, eigenfunctions)


def inverse_factor(gram):
    size = gram.shape[0]
    tiles = size // 8
    row = lax.broadcasted_iota(jnp.int32, (8, size), 0)
    column = lax.broadcasted_iota(jnp.int32, (8, size), 1)
    left = [gram[8 * i : 8 * i + 8] for i in range(tiles)]
    made = [jnp.where(row + 8 * i == column, 1.0, 0.0).astype(F32) for i in range(tiles)]
    for j in range(size):
        k, s = divmod(j, 8)
        pivot = left[k][s : s + 1, j : j + 1]
        inverse = 1.0 / pivot
        own = made[k][s : s + 1]
        scaled = left[k][s : s + 1] * inverse
        scaled_own = own * inverse
        for i in range(k, tiles):
            factor = left[i][:, j : j + 1]
            if i == k:
                if s == 7:
                    continue
                factor = jnp.where(row[:, :1] > s, factor, 0.0)
            left[i] = left[i] - factor * scaled
            made[i] = made[i] - factor * scaled_own
        made[k] = jnp.where(row == s, own * lax.rsqrt(pivot), made[k])
    return jnp.concatenate(made, axis=0)


def solve_kernel(
    points, peers, count_ref, mine_ref, other_ref, start_ref, e_ref,
    load_ref, score_ref, gain_ref, c_ref, cov_ref, held_ref, sem,
):
    samples = score_ref.shape[0]
    own, extra = samples // peers, M // peers
    size = own + extra
    core, zh = lax.axis_index("core"), lax.axis_index("zh")
    for source, ref in ((core, mine_ref), (1 - core, other_ref)):
        for half in range(2):
            base = half * peers * size
            block = jnp.concatenate(
                [ref[base + p * size : base + p * size + own] for p in range(peers)], axis=0
            )
            mean = jnp.sum(block, axis=0, keepdims=True) / samples
            place = pl.multiple_of((half * 2 + source) * 2 * M, 2 * M)
            c_ref[:, pl.ds(place, 2 * M)] = block - mean
    centred = c_ref[...]
    cov = dot(centred, centred, 0, 0, HIGHEST) / (samples - 1)
    cov_ref[...] = cov
    basis = start_ref[...]
    for _ in range(SWEEPS):
        image = dot(cov_ref[...], basis, 1, 0, HIGHEST)
        gram = dot(image, image, 0, 0, HIGHEST)
        basis = dot(image, inverse_factor(gram), 1, 1, HIGHEST)
    held_ref[...] = basis
    var = zh * 2 + core
    first = pl.multiple_of(var * 2 * M, 2 * M)
    low = held_ref[pl.ds(first, 2 * M)].astype(BF16)
    counts = local_counts(count_ref, points)
    width = STEP
    copies = []
    for v in range(2):
        for at in range(0, points, width):
            e = masked_part(e_ref[v, :, at : at + width], at, counts[v])
            load_ref_v = dot(low[v * M : (v + 1) * M], e, 0, 0).astype(BF16)
            load_ref[v, :, at : at + width] = load_ref_v
    scores = dot(c_ref[...], held_ref[...], 1, 0, HIGHEST)
    score_ref[...] = scores
    scores_low = scores.astype(BF16).astype(F32)
    base = zh * peers * size
    for v in range(2):
        outer = jnp.concatenate(
            [
                mine_ref[pl.ds(base + p * size + own, extra), v * M : (v + 1) * M]
                for p in range(peers)
            ],
            axis=0,
        )
        part = low[v * M : (v + 1) * M].astype(F32)
        square = dot(part, dot(outer, part, 1, 0, HIGHEST), 0, 0, HIGHEST)
        along = dot(c_ref[:, pl.ds(first, 2 * M)][:, v * M : (v + 1) * M], part, 1, 0, HIGHEST)
        both = scores_low * (2.0 * along - dot(scores_low, square, 1, 0, HIGHEST))
        ones = jnp.ones((8, K), F32)
        gain_ref[v : v + 1] = dot(ones, both, 1, 1, HIGHEST)[:1] / M


def solve(grid_count, mine, other, start, eigenfunctions, samples, peers):
    points = eigenfunctions.shape[2]
    joint = start.shape[0]
    vmem = pl.BlockSpec(memory_space=pltpu.VMEM)
    return pl.pallas_call(
        lambda *refs: solve_kernel(points, peers, *refs),
        name="solve",
        out_shape=(
            jax.ShapeDtypeStruct((2, K, points), BF16),
            jax.ShapeDtypeStruct((samples, K), F32),
            jax.ShapeDtypeStruct((2, samples), F32),
        ),
        in_specs=[pl.BlockSpec(memory_space=pltpu.SMEM), vmem, vmem, vmem, vmem],
        out_specs=(vmem, vmem, vmem),
        scratch_shapes=[
            pltpu.VMEM((samples, joint), F32),
            pltpu.VMEM((joint, joint), F32),
            pltpu.VMEM((joint, K), F32),
            pltpu.SemaphoreType.DMA,
        ],
        compiler_params=pltpu.CompilerParams(vmem_limit_bytes=48 << 20),
    )(grid_count, mine, other, start, eigenfunctions)


def shards(fields, eigenfunctions, start, grid_count):
    samples = fields.shape[1]
    peers = lax.axis_size("space")
    part = project(fields, eigenfunctions, grid_count, peers)
    length = part.size // peers
    tiles = lax.all_to_all(part.reshape(peers, 1, length), "space", 0, 0, tiled=True)
    tile = jnp.sum(tiles, axis=0)
    group = ("zh", "space")
    copies = jnp.broadcast_to(tile, (2 * peers, 1, length))
    mine = lax.all_to_all(copies, group, 0, 0, tiled=True).reshape(-1, 2 * M)
    other = lax.ppermute(mine, "core", ((0, 1), (1, 0)))
    return solve(grid_count, mine, other, start, eigenfunctions, samples, peers)


def solution(mesh):
    var, space = mesh.devices.shape
    finer = Mesh(mesh.devices.reshape(var // 2, 2, space), ("zh", "core", "space"))
    split = P(("zh", "core"), None, "space")
    return jax.shard_map(
        shards,
        mesh=finer,
        in_specs=(split, split, P(), P()),
        out_specs=(split, P(), P(("zh", "core"), None)),
        check_vma=False,
    )
```

profile of v0, /device:TPU:1, one launch (start us, length us, event | category | flops | bytes accessed | tf_op | source)
XLA Modules:
  0.0 107.0 jit_solution(12858235115611418799)
XLA Ops:
  0.6 0.0 copy-start
  0.6 5.8 %copy-done = bf16[2,1024,4096]{2,1,0:T(8,128)(2,1)S(1)} copy-done((bf16[2,1024,4096]{2,1,0:T(8,128)(2,1)S(1)}, bf16[2,1024,4096]{2,1,0:T(8,128)(2,1)}, u32[]{:S(2)}) %copy-start) | copy-done | bytes 16777240
  6.4 0.0 copy-start.1
  6.4 1.2 %copy-done.1 = bf16[2,64,4096]{2,1,0:T(8,128)(2,1)S(1)} copy-done((bf16[2,64,4096]{2,1,0:T(8,128)(2,1)S(1)}, bf16[2,64,4096]{2,1,0:T(8,128)(2,1)}, u32[]{:S(2)}) %copy-start.1) | copy-done | bytes 1048600
  7.6 0.0 copy-start.4
  7.6 0.7 copy-done.4
  8.3 8.2 %project.1 = f32[1088,128]{1,0:T(8,128)S(1)} custom-call(s32[8]{0:T(128)S(1)} %copy-done.4, bf16[2,1024,4096]{2,1,0:T(8,128)(2,1)S(1)} %copy-done, bf16[2,64,4096]{2,1,0:T(8,128)(2,1)S(1)} %copy-done.1), custom_call_target="tpu_custom_call" | custom-call | tf_op jit(solution)/shard_map/project/pallas_call | solution.py:66
  16.4 19.2 %all_to_all.10 = f32[32,1,4352]{2,1,0:T(1,128)S(1)} all-to-all(f32[32,1,4352]{2,1,0:T(1,128)S(1)} %bitcast.4), channel_id=1, replica_groups=mesh['zh'=2,'core'=2,'space'=32] {'space'}, dimensions={0} | all-to-all | bytes 1114112 | tf_op jit(solution)/shard_map/all_to_all | solution.py:198
  35.6 0.3 reduce_sum.9
  36.0 0.6 broadcast_in_dim.3
  36.6 0.0 copy-start.2
  36.6 0.0 copy-start.3
  36.6 0.0 copy-start.5
  36.6 24.3 %all_to_all.11 = f32[64,1,4352]{2,1,0:T(1,128)S(1)} all-to-all(f32[64,1,4352]{2,1,0:T(1,128)S(1)} %broadcast_in_dim.3), channel_id=1, replica_groups=mesh['zh'=2,'core'=2,'space'=32] {'zh','space'}, dimensions={0} | all-to-all | bytes 2228224 | tf_op jit(solution)/shard_map/all_to_all | solution.py:202
  60.9 3.9 %collective-permute-start = (f32[2176,128]{1,0:T(8,128)S(1)}, f32[2176,128]{1,0:T(8,128)S(1)}, u32[]{:S(2)}, u32[]{:S(2)}) collective-permute-start(f32[2176,128]{1,0:T(8,128)S(1)} %bitcast.2), channel_id=1, source_target_pairs={{0,32},{32,0},{1,33},{33,1},{2,34},{34,2},{3,35},{35,3},{4,36},{36... | collective-permute-start | bytes 3342344 | tf_op jit(solution)/shard_map/ppermute | solution.py:203
  64.8 2.4 %collective-permute-done.refs_2_ = f32[2176,128]{1,0:T(8,128)S(1)} collective-permute-done((f32[2176,128]{1,0:T(8,128)S(1)}, f32[2176,128]{1,0:T(8,128)S(1)}, u32[]{:S(2)}, u32[]{:S(2)}) %collective-permute-start) | collective-permute-done | bytes 1114144 | tf_op jit(solution)/shard_map/ppermute | solution.py:203
  67.2 0.0 copy-done.2
  67.2 0.0 copy-done.3
  67.2 0.0 copy-done.5
  67.2 39.7 %solve.1 = (bf16[2,128,4096]{2,1,0:T(8,128)(2,1)}, f32[1024,128]{1,0:T(8,128)}, f32[2,1024]{1,0:T(2,128)}) custom-call(s32[8]{0:T(128)S(1)} %copy-done.5, f32[2176,128]{1,0:T(8,128)S(1)} %bitcast.3, f32[2176,128]{1,0:T(8,128)S(1)} %collective-permute-done.refs_2_, f32[512,128]{1,0:T(8,128)S(1)} %copy-done.3, bf16[2,64,4096]{2,1,0:T(8,128)(2,1)S(1)} %copy-done.2), custom_call_target="tpu_custom_call" | custom-call | tf_op jit(solution)/shard_map/solve/pallas_call | solution.py:173
Async XLA Ops:
  0.6 5.8 %copy-start = (bf16[2,1024,4096]{2,1,0:T(8,128)(2,1)S(1)}, bf16[2,1024,4096]{2,1,0:T(8,128)(2,1)}, u32[]{:S(2)}) copy-start(bf16[2,1024,4096]{2,1,0:T(8,128)(2,1)} %refs_1_.1) | copy-start | bytes 50331652
  6.4 1.2 %copy-start.1 = (bf16[2,64,4096]{2,1,0:T(8,128)(2,1)S(1)}, bf16[2,64,4096]{2,1,0:T(8,128)(2,1)}, u32[]{:S(2)}) copy-start(bf16[2,64,4096]{2,1,0:T(8,128)(2,1)} %refs_4_.1) | copy-start | bytes 3145732
  7.6 0.7 copy-start.4
  36.6 30.6 %copy-start.2 = (bf16[2,64,4096]{2,1,0:T(8,128)(2,1)S(1)}, bf16[2,64,4096]{2,1,0:T(8,128)(2,1)}, u32[]{:S(2)}) copy-start(bf16[2,64,4096]{2,1,0:T(8,128)(2,1)} %refs_4_.1) | copy-start | bytes 3145732
  36.6 30.6 %copy-start.3 = (f32[512,128]{1,0:T(8,128)S(1)}, f32[512,128]{1,0:T(8,128)}, u32[]{:S(2)}) copy-start(f32[512,128]{1,0:T(8,128)} %refs_3_.1) | copy-start | bytes 786436
  36.6 30.6 %copy-start.5 = (s32[8]{0:T(128)S(1)}, s32[8]{0:T(128)}, u32[]{:S(2)}) copy-start(s32[8]{0:T(128)} %refs_0_.3) | copy-start | bytes 100
  60.9 6.2 %collective-permute-start = (f32[2176,128]{1,0:T(8,128)S(1)}, f32[2176,128]{1,0:T(8,128)S(1)}, u32[]{:S(2)}, u32[]{:S(2)}) collective-permute-start(f32[2176,128]{1,0:T(8,128)S(1)} %bitcast.2), channel_id=1, source_target_pairs={{0,32},{32,0},{1,33},{33,1},{2,34},{34,2},{3,35},{35,3},{4,36},{36... | collective-permute-start | bytes 3342344 | tf_op jit(solution)/shard_map/ppermute | solution.py:203
where the time goes:
time: 107 us
  Pallas kernels  47.8 us (45%)
  blocking collectives  43.5 us (41%)
  local copies, waits for them, and re-layouts  8.24 us (8%)
  starting transfers between devices  3.87 us (4%)
  waiting for transfers between devices  2.38 us (2%)
    pallas_call x1, Pallas kernels, solve(): pl.pallas_call(lambda *refs: solve_kernel(points, peers, *refs), name='so...  39.7 us
    all_to_all x1, blocking collectives, shards(): mine = lax.all_to_all(copies, group, 0, 0, tiled=True).reshape(-1, 2 * M)  24.3 us
    all_to_all x1, blocking collectives, shards(): lax.all_to_all(part.reshape(peers, 1, length), 'space', 0, 0, tiled=True)  19.2 us
    pallas_call x1, Pallas kernels, project(): pl.pallas_call(lambda *refs: project_kernel(points, peers, *refs), name='...  8.15 us
    unnamed x12, local copies, waits for them, and re-layouts  7.66 us
    ppermute x1, starting transfers between devices, shards(): other = lax.ppermute(mine, 'core', ((0, 1), (1, 0)))  3.87 us
    ppermute x1, waiting for transfers between devices, shards(): other = lax.ppermute(mine, 'core', ((0, 1), (1, 0)))  2.38 us
  transfers between devices with their start and end apart: 1, of which 1 were waited for; matrix products, arithmetic and copies ran while one was open for 0% of the time, Pallas kernels for 0%

commit v1 on v0

--- a/solution.py
+++ b/solution.py
@@ -11,7 +11,7 @@
 HIGHEST = lax.Precision.HIGHEST
 F32 = jnp.float32
 BF16 = jnp.bfloat16
-STEP = 512
+STEP = 1024
 
 
 def dot(left, right, lc, rc, precision=None):
@@ -78,44 +78,121 @@
             scratch_shapes=[pltpu.VMEM((rows, 2 * M), F32)],
         ),
         compiler_params=pltpu.CompilerParams(
-            dimension_semantics=("arbitrary",), vmem_limit_bytes=32 << 20
+            dimension_semantics=("arbitrary",), vmem_limit_bytes=60 << 20
         ),
     )(grid_count, fields, eigenfunctions)
 
 
-def inverse_factor(gram):
+def halves(x):
+    high = x.astype(BF16)
+    return high, (x - high.astype(F32)).astype(BF16)
+
+
+def thirds(x):
+    high, rest = x.astype(BF16), x
+    rest = rest - high.astype(F32)
+    middle = rest.astype(BF16)
+    return high, middle, (rest - middle.astype(F32)).astype(BF16)
+
+
+def folded(x):
+    half = x.shape[1] // 2
+    return x[:, :half] + x[:, half:]
+
+
+def product(left, x):
+    pair = jnp.concatenate(halves(x), axis=1)
+    return folded(dot(left, jnp.concatenate([pair, pair], axis=0), 1, 0))
+
+
+def gram_of(image):
+    high, middle, low = thirds(image)
+    pair = jnp.concatenate([high, middle], axis=1)
+    main = folded(
+        dot(jnp.concatenate([high, middle], axis=0), jnp.concatenate([pair, pair], axis=0), 0, 0)
+    )
+    last = dot(high, low, 0, 0)
+    return main + (last + last.T)
+
+
+def times_transposed(image, factor):
+    high, middle, low = thirds(image)
+    f_high, f_middle, f_low = thirds(factor)
+    right = jnp.concatenate(
+        [jnp.concatenate([f_high] * 2, axis=1), jnp.concatenate([f_middle] * 2, axis=1)], axis=0
+    )
+    main = folded(dot(jnp.concatenate([high, middle], axis=1), right, 1, 1))
+    return main + dot(
+        jnp.concatenate([high, low], axis=1), jnp.concatenate([f_low, f_high], axis=1), 1, 1
+    )
+
+
+def inverse_factor(gram, left_ref, made_ref, out_ref):
     size = gram.shape[0]
-    tiles = size // 8
-    row = lax.broadcasted_iota(jnp.int32, (8, size), 0)
-    column = lax.broadcasted_iota(jnp.int32, (8, size), 1)
-    left = [gram[8 * i : 8 * i + 8] for i in range(tiles)]
-    made = [jnp.where(row + 8 * i == column, 1.0, 0.0).astype(F32) for i in range(tiles)]
-    for j in range(size):
-        k, s = divmod(j, 8)
-        pivot = left[k][s : s + 1, j : j + 1]
-        inverse = 1.0 / pivot
-        own = made[k][s : s + 1]
-        scaled = left[k][s : s + 1] * inverse
-        scaled_own = own * inverse
-        for i in range(k, tiles):
-            factor = left[i][:, j : j + 1]
-            if i == k:
-                if s == 7:
-                    continue
-                factor = jnp.where(row[:, :1] > s, factor, 0.0)
-            left[i] = left[i] - factor * scaled
-            made[i] = made[i] - factor * scaled_own
-        made[k] = jnp.where(row == s, own * lax.rsqrt(pivot), made[k])
-    return jnp.concatenate(made, axis=0)
+    wide = (8, size)
+    row = lax.broadcasted_iota(jnp.int32, wide, 0)
+    left_ref[...] = gram
+    made_ref[...] = jnp.where(
+        lax.broadcasted_iota(jnp.int32, (size, size), 0)
+        == lax.broadcasted_iota(jnp.int32, (size, size), 1),
+        1.0,
+        0.0,
+    ).astype(F32)
+    for first in range(0, size, 16):
+        tiles = (first, first + 8)
+        left = [left_ref[t : t + 8] for t in tiles]
+        made = [made_ref[t : t + 8] for t in tiles]
+        spread = [
+            [jnp.broadcast_to(x[:, first + j : first + j + 1], wide) for j in range(16)]
+            for x in left
+        ]
+        scale = [jnp.ones(wide, F32)] * 2
+        for j in range(16):
+            tile, s = divmod(j, 8)
+            root = lax.rsqrt(jnp.broadcast_to(spread[tile][j][s : s + 1], wide))
+            scale[tile] = jnp.where(row == s, root, scale[tile])
+            inverse = root * root
+            factor = {}
+            for t in range(tile, 2):
+                factor[t] = spread[t][j] * inverse
+            factor[tile] = jnp.where(row > s, factor[tile], 0.0)
+            for other in range(j + 1, 16):
+                pivot_row = jnp.broadcast_to(spread[tile][other][s : s + 1], wide)
+                for t in factor:
+                    spread[t][other] = spread[t][other] - factor[t] * pivot_row
+            left_row = jnp.broadcast_to(left[tile][s : s + 1], wide)
+            made_row = jnp.broadcast_to(made[tile][s : s + 1], wide)
+            for t in factor:
+                left[t] = left[t] - factor[t] * left_row
+                made[t] = made[t] - factor[t] * made_row
+        upper = jnp.concatenate([left[t] * scale[t] for t in range(2)], axis=0)
+        done = jnp.concatenate([made[t] * scale[t] for t in range(2)], axis=0)
+        out_ref[first : first + 16] = done
+        rest = first + 16
+        if rest < size:
+            a, b, c = thirds(upper)
+            d, e, f = thirds(jnp.concatenate([upper, done], axis=1))
+            update = dot(
+                jnp.concatenate([a, a, b, b, a, c], axis=0),
+                jnp.concatenate([d, e, d, e, f, d], axis=0),
+                0,
+                0,
+            )
+            left_ref[rest:] = left_ref[rest:] - update[rest:, :size]
+            made_ref[rest:] = made_ref[rest:] - update[rest:, size:]
+    return out_ref[...]
 
 
 def solve_kernel(
     points, peers, count_ref, mine_ref, other_ref, start_ref, e_ref,
-    load_ref, score_ref, gain_ref, c_ref, cov_ref, held_ref, sem,
+    load_ref, score_ref, gain_ref,
+    high_ref, middle_ref, cov_ref, held_ref, left_ref, made_ref, factor_ref, out_ref, sem,
 ):
     samples = score_ref.shape[0]
+    joint = start_ref.shape[0]
     own, extra = samples // peers, M // peers
     size = own + extra
+    pair = 2 * M
     core, zh = lax.axis_index("core"), lax.axis_index("zh")
     for source, ref in ((core, mine_ref), (1 - core, other_ref)):
         for half in range(2):
@@ -124,46 +201,66 @@
                 [ref[base + p * size : base + p * size + own] for p in range(peers)], axis=0
             )
             mean = jnp.sum(block, axis=0, keepdims=True) / samples
-            place = pl.multiple_of((half * 2 + source) * 2 * M, 2 * M)
-            c_ref[:, pl.ds(place, 2 * M)] = block - mean
-    centred = c_ref[...]
-    cov = dot(centred, centred, 0, 0, HIGHEST) / (samples - 1)
-    cov_ref[...] = cov
+            place = pl.ds(pl.multiple_of((half * 2 + source) * pair, pair), pair)
+            high_ref[:, place], middle_ref[:, place] = halves(block - mean)
+    high, middle = high_ref[...], middle_ref[...]
+    main = dot(high, high, 0, 0)
+    cross = dot(high, middle, 0, 0)
+    cov = (main + (cross + cross.T)) * (1.0 / (samples - 1))
+    cov_ref[:, :joint], cov_ref[:, joint:] = halves(cov)
     basis = start_ref[...]
     for _ in range(SWEEPS):
-        image = dot(cov_ref[...], basis, 1, 0, HIGHEST)
-        gram = dot(image, image, 0, 0, HIGHEST)
-        basis = dot(image, inverse_factor(gram), 1, 1, HIGHEST)
+        image = product(cov_ref[...], basis)
+        factor = inverse_factor(gram_of(image), left_ref, made_ref, factor_ref)
+        basis = times_transposed(image, factor)
     held_ref[...] = basis
-    var = zh * 2 + core
-    first = pl.multiple_of(var * 2 * M, 2 * M)
-    low = held_ref[pl.ds(first, 2 * M)].astype(BF16)
+    first = pl.multiple_of((zh * 2 + core) * pair, pair)
+    low = held_ref[pl.ds(first, pair)].astype(BF16)
     counts = local_counts(count_ref, points)
-    width = STEP
     copies = []
-    for v in range(2):
-        for at in range(0, points, width):
-            e = masked_part(e_ref[v, :, at : at + width], at, counts[v])
-            load_ref_v = dot(low[v * M : (v + 1) * M], e, 0, 0).astype(BF16)
-            load_ref[v, :, at : at + width] = load_ref_v
-    scores = dot(c_ref[...], held_ref[...], 1, 0, HIGHEST)
+    for at in range(0, points, STEP):
+        for v in range(2):
+            e = masked_part(e_ref[v, :, at : at + STEP], at, counts[v])
+            out_ref[v, :, at : at + STEP] = dot(low[v * M : (v + 1) * M], e, 0, 0).astype(BF16)
+        part = (slice(None), slice(None), slice(at, at + STEP))
+        copy = pltpu.make_async_copy(out_ref.at[part], load_ref.at[part], sem.at[at // STEP])
+        copy.start()
+        copies.append(copy)
+    scores = product(jnp.concatenate([high_ref[...], middle_ref[...]], axis=1), basis)
     score_ref[...] = scores
-    scores_low = scores.astype(BF16).astype(F32)
+    scores_low = scores.astype(BF16)
     base = zh * peers * size
-    for v in range(2):
-        outer = jnp.concatenate(
-            [
-                mine_ref[pl.ds(base + p * size + own, extra), v * M : (v + 1) * M]
-                for p in range(peers)
-            ],
-            axis=0,
-        )
-        part = low[v * M : (v + 1) * M].astype(F32)
-        square = dot(part, dot(outer, part, 1, 0, HIGHEST), 0, 0, HIGHEST)
-        along = dot(c_ref[:, pl.ds(first, 2 * M)][:, v * M : (v + 1) * M], part, 1, 0, HIGHEST)
-        both = scores_low * (2.0 * along - dot(scores_low, square, 1, 0, HIGHEST))
-        ones = jnp.ones((8, K), F32)
-        gain_ref[v : v + 1] = dot(ones, both, 1, 1, HIGHEST)[:1] / M
+    outer = jnp.concatenate(
+        [mine_ref[pl.ds(base + p * size + own, extra)] for p in range(peers)], axis=0
+    )
+    row = lax.broadcasted_iota(jnp.int32, (pair, pair), 0) // M
+    column = lax.broadcasted_iota(jnp.int32, (pair, pair), 1) // M
+    outer = jnp.where(row == column, jnp.concatenate([outer, outer], axis=0), 0.0)
+    row = lax.broadcasted_iota(jnp.int32, (pair, 2 * K), 0) // M
+    column = lax.broadcasted_iota(jnp.int32, (pair, 2 * K), 1) // K
+    wide = low.astype(F32)
+    blocks = jnp.where(row == column, jnp.concatenate([wide, wide], axis=1), 0.0)
+    square = dot(wide, dot(outer, blocks, 1, 0, HIGHEST), 0, 0, HIGHEST)
+    square_high, square_middle = halves(-square)
+    twice = (2.0 * blocks).astype(BF16)
+    place = pl.ds(first, pair)
+    along = dot(
+        jnp.concatenate(
+            [high_ref[:, place], middle_ref[:, place], scores_low, scores_low], axis=1
+        ),
+        jnp.concatenate([twice, twice, square_high, square_middle], axis=0),
+        1,
+        0,
+    )
+    wide_scores = scores_low.astype(F32)
+    both_high, both_middle = halves(along * jnp.concatenate([wide_scores, wide_scores], axis=1))
+    chosen = lax.broadcasted_iota(jnp.int32, (8, 2 * K), 0)
+    chosen = chosen == lax.broadcasted_iota(jnp.int32, (8, 2 * K), 1) // K
+    chosen = jnp.where(chosen, 1.0, 0.0).astype(BF16)
+    gain = dot(chosen, both_high, 1, 1) + dot(chosen, both_middle, 1, 1)
+    gain_ref[...] = gain[:2] / M
+    for copy in copies:
+        copy.wait()
 
 
 def solve(grid_count, mine, other, start, eigenfunctions, samples, peers):
@@ -179,14 +276,19 @@
             jax.ShapeDtypeStruct((2, samples), F32),
         ),
         in_specs=[pl.BlockSpec(memory_space=pltpu.SMEM), vmem, vmem, vmem, vmem],
-        out_specs=(vmem, vmem, vmem),
+        out_specs=(pl.BlockSpec(memory_space=pl.ANY), vmem, vmem),
         scratch_shapes=[
-            pltpu.VMEM((samples, joint), F32),
-            pltpu.VMEM((joint, joint), F32),
+            pltpu.VMEM((samples, joint), BF16),
+            pltpu.VMEM((samples, joint), BF16),
+            pltpu.VMEM((joint, 2 * joint), BF16),
             pltpu.VMEM((joint, K), F32),
-            pltpu.SemaphoreType.DMA,
+            pltpu.VMEM((K, K), F32),
+            pltpu.VMEM((K, K), F32),
+            pltpu.VMEM((K, K), F32),
+            pltpu.VMEM((2, K, points), BF16),
+            pltpu.SemaphoreType.DMA((points // STEP,)),
         ],
-        compiler_params=pltpu.CompilerParams(vmem_limit_bytes=48 << 20),
+        compiler_params=pltpu.CompilerParams(vmem_limit_bytes=40 << 20),
     )(grid_count, mine, other, start, eigenfunctions)
 
 

time: 107 us -> 77.8 us (0.73)
  Pallas kernels: 47.8 us -> 25.8 us
  local copies, waits for them, and re-layouts: 8.24 us -> 0.59 us
    pallas_call x1, Pallas kernels: 39.7 us -> 15.5 us  [solve(): pl.pallas_call(lambda *refs: solve_kernel(points, peers, *refs), name='so...]
    unnamed x12 -> x6, local copies, waits for them, and re-layouts: 7.66 us -> 0.02 us
    pallas_call x1, Pallas kernels: 8.15 us -> 10.3 us  [project(): pl.pallas_call(lambda *refs: project_kernel(points, peers, *refs), name='...]
where the time goes in v1:
time: 77.8 us; the launch traced here: 77.5 us
  blocking collectives  43.7 us (56%)
  Pallas kernels  25.8 us (33%)
  starting transfers between devices  3.87 us (5%)
  waiting for transfers between devices  2.38 us (3%)
  between operations  0.83 us (1%)
    all_to_all x1, blocking collectives, shards(): mine = lax.all_to_all(copies, group, 0, 0, tiled=True).reshape(-1, 2 * M)  24.3 us
    all_to_all x1, blocking collectives, shards(): lax.all_to_all(part.reshape(peers, 1, length), 'space', 0, 0, tiled=True)  19.4 us
    pallas_call x1, Pallas kernels, solve(): pl.pallas_call(lambda *refs: solve_kernel(points, peers, *refs), name='so...  15.5 us
    pallas_call x1, Pallas kernels, project(): pl.pallas_call(lambda *refs: project_kernel(points, peers, *refs), name='...  10.3 us
    ppermute x1, starting transfers between devices, shards(): other = lax.ppermute(mine, 'core', ((0, 1), (1, 0)))  3.87 us
    ppermute x1, waiting for transfers between devices, shards(): other = lax.ppermute(mine, 'core', ((0, 1), (1, 0)))  2.38 us
  transfers between devices with their start and end apart: 1, of which 1 were waited for; matrix products, arithmetic and copies ran while one was open for 0% of the time, Pallas kernels for 0%

profile of v1, /device:TPU:1, one launch (start us, length us, event | category | flops | bytes accessed | tf_op | source)
XLA Modules:
  0.0 77.5 jit_solution(14202524764839272311)
XLA Ops:
  0.6 10.3 %project.1 = f32[1088,128]{1,0:T(8,128)} custom-call(s32[8]{0:T(128)} %refs_0_.3, bf16[2,1024,4096]{2,1,0:T(8,128)(2,1)} %refs_1_.1, bf16[2,64,4096]{2,1,0:T(8,128)(2,1)} %refs_4_.1), custom_call_target="tpu_custom_call" | custom-call | tf_op jit(solution)/shard_map/project/pallas_call | solution.py:66
  10.9 19.4 %all_to_all.10 = f32[32,1,4352]{2,1,0:T(1,128)S(1)} all-to-all(f32[32,1,4352]{2,1,0:T(1,128)} %bitcast.4), channel_id=1, replica_groups=mesh['zh'=2,'core'=2,'space'=32] {'space'}, dimensions={0} | all-to-all | bytes 1114112 | tf_op jit(solution)/shard_map/all_to_all | solution.py:300
  30.3 0.3 reduce_sum.9
  30.6 0.6 broadcast_in_dim.3
  31.2 0.0 copy-start
  31.2 0.0 copy-start.1
  31.2 0.0 copy-start.2
  31.3 24.3 %all_to_all.11 = f32[64,1,4352]{2,1,0:T(1,128)S(1)} all-to-all(f32[64,1,4352]{2,1,0:T(1,128)S(1)} %broadcast_in_dim.3), channel_id=1, replica_groups=mesh['zh'=2,'core'=2,'space'=32] {'zh','space'}, dimensions={0} | all-to-all | bytes 2228224 | tf_op jit(solution)/shard_map/all_to_all | solution.py:304
  55.6 3.9 %collective-permute-start = (f32[2176,128]{1,0:T(8,128)S(1)}, f32[2176,128]{1,0:T(8,128)S(1)}, u32[]{:S(2)}, u32[]{:S(2)}) collective-permute-start(f32[2176,128]{1,0:T(8,128)S(1)} %bitcast.2), channel_id=1, source_target_pairs={{0,32},{32,0},{1,33},{33,1},{2,34},{34,2},{3,35},{35,3},{4,36},{36... | collective-permute-start | bytes 3342344 | tf_op jit(solution)/shard_map/ppermute | solution.py:305
  59.5 2.4 %collective-permute-done.refs_2_ = f32[2176,128]{1,0:T(8,128)S(1)} collective-permute-done((f32[2176,128]{1,0:T(8,128)S(1)}, f32[2176,128]{1,0:T(8,128)S(1)}, u32[]{:S(2)}, u32[]{:S(2)}) %collective-permute-start) | collective-permute-done | bytes 1114144 | tf_op jit(solution)/shard_map/ppermute | solution.py:305
  61.9 0.0 copy-done
  61.9 0.0 copy-done.1
  61.9 0.0 copy-done.2
  61.9 15.5 %solve.1 = (bf16[2,128,4096]{2,1,0:T(8,128)(2,1)}, f32[1024,128]{1,0:T(8,128)}, f32[2,1024]{1,0:T(2,128)}) custom-call(s32[8]{0:T(128)S(1)} %copy-done.2, f32[2176,128]{1,0:T(8,128)S(1)} %bitcast.3, f32[2176,128]{1,0:T(8,128)S(1)} %collective-permute-done.refs_2_, f32[512,128]{1,0:T(8,128)S(1)} %copy-done.1, bf16[2,64,4096]{2,1,0:T(8,128)(2,1)S(1)} %copy-done), custom_call_target="tpu_custom_call" | custom-call | tf_op jit(solution)/shard_map/solve/pallas_call | solution.py:270
Async XLA Ops:
  31.2 30.6 %copy-start = (bf16[2,64,4096]{2,1,0:T(8,128)(2,1)S(1)}, bf16[2,64,4096]{2,1,0:T(8,128)(2,1)}, u32[]{:S(2)}) copy-start(bf16[2,64,4096]{2,1,0:T(8,128)(2,1)} %refs_4_.1) | copy-start | bytes 3145732
  31.2 30.6 %copy-start.1 = (f32[512,128]{1,0:T(8,128)S(1)}, f32[512,128]{1,0:T(8,128)}, u32[]{:S(2)}) copy-start(f32[512,128]{1,0:T(8,128)} %refs_3_.1) | copy-start | bytes 786436
  31.2 30.6 %copy-start.2 = (s32[8]{0:T(128)S(1)}, s32[8]{0:T(128)}, u32[]{:S(2)}) copy-start(s32[8]{0:T(128)} %refs_0_.3) | copy-start | bytes 100
  55.6 6.2 %collective-permute-start = (f32[2176,128]{1,0:T(8,128)S(1)}, f32[2176,128]{1,0:T(8,128)S(1)}, u32[]{:S(2)}, u32[]{:S(2)}) collective-permute-start(f32[2176,128]{1,0:T(8,128)S(1)} %bitcast.2), channel_id=1, source_target_pairs={{0,32},{32,0},{1,33},{33,1},{2,34},{34,2},{3,35},{35,3},{4,36},{36... | collective-permute-start | bytes 3342344 | tf_op jit(solution)/shard_map/ppermute | solution.py:305

commit v2 on v1

--- a/solution.py
+++ b/solution.py
@@ -100,8 +100,11 @@
     return x[:, :half] + x[:, half:]
 
 
-def product(left, x):
-    pair = jnp.concatenate(halves(x), axis=1)
+def pair_up(x):
+    return jnp.concatenate(halves(x), axis=1)
+
+
+def product(left, pair):
     return folded(dot(left, jnp.concatenate([pair, pair], axis=0), 1, 0))
 
 
@@ -184,7 +187,7 @@
 
 
 def solve_kernel(
-    points, peers, count_ref, mine_ref, other_ref, start_ref, e_ref,
+    points, peers, mine_ref, other_ref, start_ref, e_ref,
     load_ref, score_ref, gain_ref,
     high_ref, middle_ref, cov_ref, held_ref, left_ref, made_ref, factor_ref, out_ref, sem,
 ):
@@ -208,25 +211,25 @@
     cross = dot(high, middle, 0, 0)
     cov = (main + (cross + cross.T)) * (1.0 / (samples - 1))
     cov_ref[:, :joint], cov_ref[:, joint:] = halves(cov)
-    basis = start_ref[...]
+    basis_pair = start_ref[...]
     for _ in range(SWEEPS):
-        image = product(cov_ref[...], basis)
+        image = product(cov_ref[...], basis_pair)
         factor = inverse_factor(gram_of(image), left_ref, made_ref, factor_ref)
         basis = times_transposed(image, factor)
+        basis_pair = pair_up(basis)
     held_ref[...] = basis
     first = pl.multiple_of((zh * 2 + core) * pair, pair)
     low = held_ref[pl.ds(first, pair)].astype(BF16)
-    counts = local_counts(count_ref, points)
     copies = []
     for at in range(0, points, STEP):
         for v in range(2):
-            e = masked_part(e_ref[v, :, at : at + STEP], at, counts[v])
+            e = e_ref[v, :, at : at + STEP]
             out_ref[v, :, at : at + STEP] = dot(low[v * M : (v + 1) * M], e, 0, 0).astype(BF16)
         part = (slice(None), slice(None), slice(at, at + STEP))
         copy = pltpu.make_async_copy(out_ref.at[part], load_ref.at[part], sem.at[at // STEP])
         copy.start()
         copies.append(copy)
-    scores = product(jnp.concatenate([high_ref[...], middle_ref[...]], axis=1), basis)
+    scores = product(jnp.concatenate([high_ref[...], middle_ref[...]], axis=1), basis_pair)
     score_ref[...] = scores
     scores_low = scores.astype(BF16)
     base = zh * peers * size
@@ -263,8 +266,8 @@
         copy.wait()
 
 
-def solve(grid_count, mine, other, start, eigenfunctions, samples, peers):
-    points = eigenfunctions.shape[2]
+def solve(mine, other, start, masked, samples, peers):
+    points = masked.shape[2]
     joint = start.shape[0]
     vmem = pl.BlockSpec(memory_space=pltpu.VMEM)
     return pl.pallas_call(
@@ -275,7 +278,7 @@
             jax.ShapeDtypeStruct((samples, K), F32),
             jax.ShapeDtypeStruct((2, samples), F32),
         ),
-        in_specs=[pl.BlockSpec(memory_space=pltpu.SMEM), vmem, vmem, vmem, vmem],
+        in_specs=[vmem] * 4,
         out_specs=(pl.BlockSpec(memory_space=pl.ANY), vmem, vmem),
         scratch_shapes=[
             pltpu.VMEM((samples, joint), BF16),
@@ -289,7 +292,73 @@
             pltpu.SemaphoreType.DMA((points // STEP,)),
         ],
         compiler_params=pltpu.CompilerParams(vmem_limit_bytes=40 << 20),
-    )(grid_count, mine, other, start, eigenfunctions)
+    )(mine, other, start, masked)
+
+
+def mask_kernel(points, count_ref, e_ref, after_ref, out_ref):
+    counts = local_counts(count_ref, points)
+    for v in range(2):
+        out_ref[v] = masked_part(e_ref[v], 0, counts[v])
+
+
+def mask(grid_count, eigenfunctions, after):
+    vmem = pl.BlockSpec(memory_space=pltpu.VMEM)
+    points = eigenfunctions.shape[2]
+    return pl.pallas_call(
+        lambda *refs: mask_kernel(points, *refs),
+        name="mask",
+        out_shape=jax.ShapeDtypeStruct(eigenfunctions.shape, BF16),
+        in_specs=[pl.BlockSpec(memory_space=pltpu.SMEM), vmem, pl.BlockSpec(memory_space=pl.ANY)],
+        out_specs=vmem,
+        compiler_params=pltpu.CompilerParams(vmem_limit_bytes=8 << 20),
+        cost_estimate=pl.CostEstimate(
+            flops=eigenfunctions.size, bytes_accessed=4 * eigenfunctions.size, transcendentals=0
+        ),
+    )(grid_count, eigenfunctions, after)
+
+
+def pair_kernel(x_ref, after_ref, out_ref):
+    out_ref[:, :K], out_ref[:, K:] = halves(x_ref[...])
+
+
+def pair_of(x, after):
+    vmem = pl.BlockSpec(memory_space=pltpu.VMEM)
+    return pl.pallas_call(
+        pair_kernel,
+        name="pair",
+        out_shape=jax.ShapeDtypeStruct((x.shape[0], 2 * K), BF16),
+        in_specs=[vmem, pl.BlockSpec(memory_space=pl.ANY)],
+        out_specs=vmem,
+        compiler_params=pltpu.CompilerParams(vmem_limit_bytes=4 << 20),
+        cost_estimate=pl.CostEstimate(
+            flops=4 * x.size, bytes_accessed=8 * x.size, transcendentals=0
+        ),
+    )(x, after)
+
+
+def spread_kernel(peers, copies, tiles_ref, after_ref, out_ref):
+    size = tiles_ref.shape[0] // peers
+    total = tiles_ref[:size]
+    for peer in range(1, peers):
+        total = total + tiles_ref[peer * size : (peer + 1) * size]
+    for copy in range(copies):
+        out_ref[copy * size : (copy + 1) * size] = total
+
+
+def spread(tiles, after, peers, copies):
+    vmem = pl.BlockSpec(memory_space=pltpu.VMEM)
+    rows, columns = tiles.shape
+    return pl.pallas_call(
+        lambda *refs: spread_kernel(peers, copies, *refs),
+        name="spread",
+        out_shape=jax.ShapeDtypeStruct((rows // peers * copies, columns), F32),
+        in_specs=[vmem, pl.BlockSpec(memory_space=pl.ANY)],
+        out_specs=vmem,
+        compiler_params=pltpu.CompilerParams(vmem_limit_bytes=8 << 20),
+        cost_estimate=pl.CostEstimate(
+            flops=tiles.size, bytes_accessed=12 * tiles.size, transcendentals=0
+        ),
+    )(tiles, after)
 
 
 def shards(fields, eigenfunctions, start, grid_count):
@@ -298,12 +367,14 @@
     part = project(fields, eigenfunctions, grid_count, peers)
     length = part.size // peers
     tiles = lax.all_to_all(part.reshape(peers, 1, length), "space", 0, 0, tiled=True)
-    tile = jnp.sum(tiles, axis=0)
-    group = ("zh", "space")
-    copies = jnp.broadcast_to(tile, (2 * peers, 1, length))
-    mine = lax.all_to_all(copies, group, 0, 0, tiled=True).reshape(-1, 2 * M)
+    masked = mask(grid_count, eigenfunctions, part)
+    copies = spread(tiles.reshape(-1, 2 * M), masked, peers, 2 * peers)
+    sent = copies.reshape(2 * peers, 1, length)
+    mine = lax.all_to_all(sent, ("zh", "space"), 0, 0, tiled=True).reshape(-1, 2 * M)
+    first = pair_of(start, copies)
+    mine, first = lax.optimization_barrier((mine, first))
     other = lax.ppermute(mine, "core", ((0, 1), (1, 0)))
-    return solve(grid_count, mine, other, start, eigenfunctions, samples, peers)
+    return solve(mine, other, first, masked, samples, peers)
 
 
 def solution(mesh):

time: 77.8 us -> 78 us (level)
  blocking collectives: 43.7 us -> 0 us
  waiting for transfers between devices: 2.38 us -> 28.1 us
  starting transfers between devices: 3.87 us -> 21.3 us
  Pallas kernels: 25.8 us -> 27.4 us
    all_to_all x2 -> x0, blocking collectives: 43.7 us -> none  [the longest x1 24.3 us: shards(): mine = lax.all_to_all(copies, group, 0, 0, tiled=True).reshape(-1, 2 * M)]
    all_to_all x0 -> x2, waiting for transfers between devices: none -> 25.7 us  [the longest x1 16.4 us: shards(): lax.all_to_all(sent, ('zh', 'space'), 0, 0, tiled=True).reshape(-1, 2 * M)]
    all_to_all x0 -> x2, starting transfers between devices: none -> 17.4 us  [the longest x1 9.36 us: shards(): lax.all_to_all(part.reshape(peers, 1, length), 'space', 0, 0, tiled=True)]
    pallas_call x0 -> x3, Pallas kernels: none -> 1.95 us  [the longest x1 1.11 us: spread(): pl.pallas_call(lambda *refs: spread_kernel(peers, copies, *refs), name='s...]
  transfers between devices with their start and end apart: 1 -> 3, of which waited for: 1 -> 3; matrix products, arithmetic and copies ran while one was open for 0% -> 0% of each run, Pallas kernels for 0% -> 1%
where the time goes in v2:
time: 78 us; the launch traced here: 77.6 us
  waiting for transfers between devices  28.1 us (36%)
  Pallas kernels  27.4 us (35%)
  starting transfers between devices  21.3 us (27%)
  between operations  0.87 us (1%)
    all_to_all x1, waiting for transfers between devices, shards(): lax.all_to_all(sent, ('zh', 'space'), 0, 0, tiled=True).reshape(-1, 2 * M)  16.4 us
    pallas_call x1, Pallas kernels, solve(): pl.pallas_call(lambda *refs: solve_kernel(points, peers, *refs), name='so...  15 us
    pallas_call x1, Pallas kernels, project(): pl.pallas_call(lambda *refs: project_kernel(points, peers, *refs), name='...  10.4 us
    all_to_all x1, starting transfers between devices, shards(): lax.all_to_all(part.reshape(peers, 1, length), 'space', 0, 0, tiled=True)  9.36 us
    all_to_all x1, waiting for transfers between devices, shards(): lax.all_to_all(part.reshape(peers, 1, length), 'space', 0, 0, tiled=True)  9.32 us
    all_to_all x1, starting transfers between devices, shards(): lax.all_to_all(sent, ('zh', 'space'), 0, 0, tiled=True).reshape(-1, 2 * M)  8.05 us
    ppermute x1, starting transfers between devices, shards(): other = lax.ppermute(mine, 'core', ((0, 1), (1, 0)))  3.87 us
    ppermute x1, waiting for transfers between devices, shards(): other = lax.ppermute(mine, 'core', ((0, 1), (1, 0)))  2.38 us
  transfers between devices with their start and end apart: 3, of which 3 were waited for; matrix products, arithmetic and copies ran while one was open for 0% of the time, Pallas kernels for 1%

profile of v2, /device:TPU:1, one launch (start us, length us, event | category | flops | bytes accessed | tf_op | source)
XLA Modules:
  0.0 77.6 jit_solution(11424264716571842212)
XLA Ops:
  0.6 0.0 copy-start.1
  0.6 10.4 %project.1.refs_2_ = f32[1088,128]{1,0:T(8,128)} custom-call(s32[8]{0:T(128)} %refs_0_.3, bf16[2,1024,4096]{2,1,0:T(8,128)(2,1)} %refs_1_.2, bf16[2,64,4096]{2,1,0:T(8,128)(2,1)} %refs_1_.3), custom_call_target="tpu_custom_call" | custom-call | tf_op jit(solution)/shard_map/project/pallas_call | solution.py:66
  11.1 0.0 copy-start
  11.1 0.0 copy-start.3
  11.1 9.4 %all-to-all-start = ((f32[32,1,4352]{2,1,0:T(1,128)}), f32[32,1,4352]{2,1,0:T(1,128)S(1)}, u32[]{:S(2)}, u32[]{:S(2)}) async-start(f32[32,1,4352]{2,1,0:T(1,128)} %bitcast.4), calls=%async_computation | async-start | bytes 1114112 | tf_op jit(solution)/shard_map/all_to_all | solution.py:369
  20.5 0.0 copy-done.1
  20.5 0.0 copy-done
  20.5 0.0 copy-done.3
  20.5 0.8 %mask.1.refs_1_.refs_3_ = bf16[2,64,4096]{2,1,0:T(8,128)(2,1)S(1)} custom-call(s32[8]{0:T(128)S(1)} %copy-done.3, bf16[2,64,4096]{2,1,0:T(8,128)(2,1)S(1)} %copy-done.1, f32[1088,128]{1,0:T(8,128)S(1)} %copy-done), custom_call_target="tpu_custom_call" | custom-call | flops 524288 | bytes 2097152 | tf_op jit(solution)/shard_map/mask/pallas_call | solution.py:307
  21.3 9.3 %all-to-all-done = f32[32,1,4352]{2,1,0:T(1,128)S(1)} async-done(((f32[32,1,4352]{2,1,0:T(1,128)}), f32[32,1,4352]{2,1,0:T(1,128)S(1)}, u32[]{:S(2)}, u32[]{:S(2)}) %all-to-all-start) | async-done | bytes 557088 | tf_op jit(solution)/shard_map/all_to_all | solution.py:369
  30.6 1.1 %spread.1.after_ref = f32[2176,128]{1,0:T(8,128)} custom-call(f32[1088,128]{1,0:T(8,128)S(1)} %bitcast.7, bf16[2,64,4096]{2,1,0:T(8,128)(2,1)S(1)} %mask.1.refs_1_.refs_3_), custom_call_target="tpu_custom_call" | custom-call | flops 139264 | bytes 1671168 | tf_op jit(solution)/shard_map/spread/pallas_call | solution.py:351
  31.7 0.0 copy-start.2
  31.7 8.1 %all-to-all-start.1 = ((f32[64,1,4352]{2,1,0:T(1,128)}), f32[64,1,4352]{2,1,0:T(1,128)S(1)}, u32[]{:S(2)}, u32[]{:S(2)}) async-start(f32[64,1,4352]{2,1,0:T(1,128)} %bitcast.2), calls=%async_computation.1 | async-start | bytes 2228224 | tf_op jit(solution)/shard_map/all_to_all | solution.py:373
  39.8 0.0 copy-done.2
  39.8 0.1 pair.1.refs_2_
  39.8 16.4 %all-to-all-done.1 = f32[64,1,4352]{2,1,0:T(1,128)S(1)} async-done(((f32[64,1,4352]{2,1,0:T(1,128)}), f32[64,1,4352]{2,1,0:T(1,128)S(1)}, u32[]{:S(2)}, u32[]{:S(2)}) %all-to-all-start.1) | async-done | bytes 1114144 | tf_op jit(solution)/shard_map/all_to_all | solution.py:373
  56.3 3.9 %collective-permute-start = (f32[2176,128]{1,0:T(8,128)S(1)}, f32[2176,128]{1,0:T(8,128)S(1)}, u32[]{:S(2)}, u32[]{:S(2)}) collective-permute-start(f32[2176,128]{1,0:T(8,128)S(1)} %bitcast.5), channel_id=1, source_target_pairs={{0,32},{32,0},{1,33},{33,1},{2,34},{34,2},{3,35},{35,3},{4,36},{36... | collective-permute-start | bytes 3342344 | tf_op jit(solution)/shard_map/ppermute | solution.py:376
  60.1 2.4 %collective-permute-done.refs_1_ = f32[2176,128]{1,0:T(8,128)S(1)} collective-permute-done((f32[2176,128]{1,0:T(8,128)S(1)}, f32[2176,128]{1,0:T(8,128)S(1)}, u32[]{:S(2)}, u32[]{:S(2)}) %collective-permute-start) | collective-permute-done | bytes 1114144 | tf_op jit(solution)/shard_map/ppermute | solution.py:376
  62.5 15.0 %solve.1 = (bf16[2,128,4096]{2,1,0:T(8,128)(2,1)}, f32[1024,128]{1,0:T(8,128)}, f32[2,1024]{1,0:T(2,128)}) custom-call(f32[2176,128]{1,0:T(8,128)S(1)} %bitcast.6, f32[2176,128]{1,0:T(8,128)S(1)} %collective-permute-done.refs_1_, bf16[512,256]{1,0:T(8,128)(2,1)S(1)} %pair.1.refs_2_, bf16[2,64,4096]{2,1,0:T(8,128)(2,1)S(1)} %mask.1.refs_1_.refs_3_), custom_call_target="tpu_custom_call" | custom-call | tf_op jit(solution)/shard_map/solve/pallas_call | solution.py:273
Async XLA Ops:
  0.6 19.8 %copy-start.1 = (bf16[2,64,4096]{2,1,0:T(8,128)(2,1)S(1)}, bf16[2,64,4096]{2,1,0:T(8,128)(2,1)}, u32[]{:S(2)}) copy-start(bf16[2,64,4096]{2,1,0:T(8,128)(2,1)} %refs_1_.3) | copy-start | bytes 3145732
  11.1 9.4 %copy-start = (f32[1088,128]{1,0:T(8,128)S(1)}, f32[1088,128]{1,0:T(8,128)}, u32[]{:S(2)}) copy-start(f32[1088,128]{1,0:T(8,128)} %project.1.refs_2_) | copy-start | bytes 1671172
  11.1 9.4 %copy-start.3 = (s32[8]{0:T(128)S(1)}, s32[8]{0:T(128)}, u32[]{:S(2)}) copy-start(s32[8]{0:T(128)} %refs_0_.3) | copy-start | bytes 100
  11.1 19.5 %all-to-all-start = ((f32[32,1,4352]{2,1,0:T(1,128)}), f32[32,1,4352]{2,1,0:T(1,128)S(1)}, u32[]{:S(2)}, u32[]{:S(2)}) async-start(f32[32,1,4352]{2,1,0:T(1,128)} %bitcast.4), calls=%async_computation | async-start | bytes 1114112 | tf_op jit(solution)/shard_map/all_to_all | solution.py:369
  31.7 8.1 %copy-start.2 = (f32[512,128]{1,0:T(8,128)S(1)}, f32[512,128]{1,0:T(8,128)}, u32[]{:S(2)}) copy-start(f32[512,128]{1,0:T(8,128)} %x_ref.1) | copy-start | bytes 786436
  31.7 24.5 %all-to-all-start.1 = ((f32[64,1,4352]{2,1,0:T(1,128)}), f32[64,1,4352]{2,1,0:T(1,128)S(1)}, u32[]{:S(2)}, u32[]{:S(2)}) async-start(f32[64,1,4352]{2,1,0:T(1,128)} %bitcast.2), calls=%async_computation.1 | async-start | bytes 2228224 | tf_op jit(solution)/shard_map/all_to_all | solution.py:373
  56.3 6.2 %collective-permute-start = (f32[2176,128]{1,0:T(8,128)S(1)}, f32[2176,128]{1,0:T(8,128)S(1)}, u32[]{:S(2)}, u32[]{:S(2)}) collective-permute-start(f32[2176,128]{1,0:T(8,128)S(1)} %bitcast.5), channel_id=1, source_target_pairs={{0,32},{32,0},{1,33},{33,1},{2,34},{34,2},{3,35},{35,3},{4,36},{36... | collective-permute-start | bytes 3342344 | tf_op jit(solution)/shard_map/ppermute | solution.py:376

commit v3 on v2

--- a/solution.py
+++ b/solution.py
@@ -12,6 +12,7 @@
 F32 = jnp.float32
 BF16 = jnp.bfloat16
 STEP = 1024
+BLOCK = 32
 
 
 def dot(left, right, lc, rc, precision=None):
@@ -141,39 +142,41 @@
         1.0,
         0.0,
     ).astype(F32)
-    for first in range(0, size, 16):
-        tiles = (first, first + 8)
-        left = [left_ref[t : t + 8] for t in tiles]
-        made = [made_ref[t : t + 8] for t in tiles]
+    for first in range(0, size, BLOCK):
+        starts = range(first, first + BLOCK, 8)
+        left = [left_ref[t : t + 8] for t in starts]
+        made = [made_ref[t : t + 8] for t in starts]
         spread = [
-            [jnp.broadcast_to(x[:, first + j : first + j + 1], wide) for j in range(16)]
-            for x in left
+            [
+                jnp.broadcast_to(x[:, first + j : first + j + 1], wide)
+                for j in range(8 * t + 8)
+            ]
+            for t, x in enumerate(left)
         ]
-        scale = [jnp.ones(wide, F32)] * 2
-        for j in range(16):
+        scale = [jnp.ones(wide, F32)] * len(left)
+        for j in range(BLOCK):
             tile, s = divmod(j, 8)
             root = lax.rsqrt(jnp.broadcast_to(spread[tile][j][s : s + 1], wide))
             scale[tile] = jnp.where(row == s, root, scale[tile])
             inverse = root * root
-            factor = {}
-            for t in range(tile, 2):
-                factor[t] = spread[t][j] * inverse
+            factor = {t: spread[t][j] * inverse for t in range(tile, len(left))}
             factor[tile] = jnp.where(row > s, factor[tile], 0.0)
-            for other in range(j + 1, 16):
-                pivot_row = jnp.broadcast_to(spread[tile][other][s : s + 1], wide)
-                for t in factor:
-                    spread[t][other] = spread[t][other] - factor[t] * pivot_row
+            for other in range(j + 1, BLOCK):
+                home, at = divmod(other, 8)
+                entry = jnp.broadcast_to(spread[home][j][at : at + 1], wide)
+                for t in range(home, len(left)):
+                    spread[t][other] = spread[t][other] - factor[t] * entry
             left_row = jnp.broadcast_to(left[tile][s : s + 1], wide)
             made_row = jnp.broadcast_to(made[tile][s : s + 1], wide)
             for t in factor:
                 left[t] = left[t] - factor[t] * left_row
                 made[t] = made[t] - factor[t] * made_row
-        upper = jnp.concatenate([left[t] * scale[t] for t in range(2)], axis=0)
-        done = jnp.concatenate([made[t] * scale[t] for t in range(2)], axis=0)
-        out_ref[first : first + 16] = done
-        rest = first + 16
+        upper = jnp.concatenate([x * y for x, y in zip(left, scale)], axis=0)
+        done = jnp.concatenate([x * y for x, y in zip(made, scale)], axis=0)
+        out_ref[first : first + BLOCK] = done
+        rest = first + BLOCK
         if rest < size:
-            a, b, c = thirds(upper)
+            a, b, c = thirds(upper[:, rest:])
             d, e, f = thirds(jnp.concatenate([upper, done], axis=1))
             update = dot(
                 jnp.concatenate([a, a, b, b, a, c], axis=0),
@@ -181,17 +184,17 @@
                 0,
                 0,
             )
-            left_ref[rest:] = left_ref[rest:] - update[rest:, :size]
-            made_ref[rest:] = made_ref[rest:] - update[rest:, size:]
+            left_ref[rest:] = left_ref[rest:] - update[:, :size]
+            made_ref[rest:] = made_ref[rest:] - update[:, size:]
     return out_ref[...]
 
 
 def solve_kernel(
     points, peers, mine_ref, other_ref, start_ref, e_ref,
     load_ref, score_ref, gain_ref,
-    high_ref, middle_ref, cov_ref, held_ref, left_ref, made_ref, factor_ref, out_ref, sem,
+    high_ref, middle_ref, cov_ref, held_ref, left_ref, made_ref, factor_ref, out_ref, score_out_ref, sem, score_sem,
 ):
-    samples = score_ref.shape[0]
+    samples = gain_ref.shape[1]
     joint = start_ref.shape[0]
     own, extra = samples // peers, M // peers
     size = own + extra
@@ -230,7 +233,10 @@
         copy.start()
         copies.append(copy)
     scores = product(jnp.concatenate([high_ref[...], middle_ref[...]], axis=1), basis_pair)
-    score_ref[...] = scores
+    score_out_ref[...] = scores
+    copy = pltpu.make_async_copy(score_out_ref, score_ref, score_sem)
+    copy.start()
+    copies.append(copy)
     scores_low = scores.astype(BF16)
     base = zh * peers * size
     outer = jnp.concatenate(
@@ -279,7 +285,7 @@
             jax.ShapeDtypeStruct((2, samples), F32),
         ),
         in_specs=[vmem] * 4,
-        out_specs=(pl.BlockSpec(memory_space=pl.ANY), vmem, vmem),
+        out_specs=(pl.BlockSpec(memory_space=pl.ANY), pl.BlockSpec(memory_space=pl.ANY), vmem),
         scratch_shapes=[
             pltpu.VMEM((samples, joint), BF16),
             pltpu.VMEM((samples, joint), BF16),
@@ -289,7 +295,9 @@
             pltpu.VMEM((K, K), F32),
             pltpu.VMEM((K, K), F32),
             pltpu.VMEM((2, K, points), BF16),
+            pltpu.VMEM((samples, K), F32),
             pltpu.SemaphoreType.DMA((points // STEP,)),
+            pltpu.SemaphoreType.DMA,
         ],
         compiler_params=pltpu.CompilerParams(vmem_limit_bytes=40 << 20),
     )(mine, other, start, masked)
@@ -336,31 +344,6 @@
     )(x, after)
 
 
-def spread_kernel(peers, copies, tiles_ref, after_ref, out_ref):
-    size = tiles_ref.shape[0] // peers
-    total = tiles_ref[:size]
-    for peer in range(1, peers):
-        total = total + tiles_ref[peer * size : (peer + 1) * size]
-    for copy in range(copies):
-        out_ref[copy * size : (copy + 1) * size] = total
-
-
-def spread(tiles, after, peers, copies):
-    vmem = pl.BlockSpec(memory_space=pltpu.VMEM)
-    rows, columns = tiles.shape
-    return pl.pallas_call(
-        lambda *refs: spread_kernel(peers, copies, *refs),
-        name="spread",
-        out_shape=jax.ShapeDtypeStruct((rows // peers * copies, columns), F32),
-        in_specs=[vmem, pl.BlockSpec(memory_space=pl.ANY)],
-        out_specs=vmem,
-        compiler_params=pltpu.CompilerParams(vmem_limit_bytes=8 << 20),
-        cost_estimate=pl.CostEstimate(
-            flops=tiles.size, bytes_accessed=12 * tiles.size, transcendentals=0
-        ),
-    )(tiles, after)
-
-
 def shards(fields, eigenfunctions, start, grid_count):
     samples = fields.shape[1]
     peers = lax.axis_size("space")
@@ -368,11 +351,10 @@
     length = part.size // peers
     tiles = lax.all_to_all(part.reshape(peers, 1, length), "space", 0, 0, tiled=True)
     masked = mask(grid_count, eigenfunctions, part)
-    copies = spread(tiles.reshape(-1, 2 * M), masked, peers, 2 * peers)
-    sent = copies.reshape(2 * peers, 1, length)
-    mine = lax.all_to_all(sent, ("zh", "space"), 0, 0, tiled=True).reshape(-1, 2 * M)
-    first = pair_of(start, copies)
-    mine, first = lax.optimization_barrier((mine, first))
+    tile = jnp.sum(tiles, axis=0)
+    copies = jnp.broadcast_to(tile, (2 * peers, 1, length))
+    mine = lax.all_to_all(copies, ("zh", "space"), 0, 0, tiled=True).reshape(-1, 2 * M)
+    first = pair_of(start, tile)
     other = lax.ppermute(mine, "core", ((0, 1), (1, 0)))
     return solve(mine, other, first, masked, samples, peers)
 

time: 78 us -> 77 us (0.987)
  blocking collectives: 0 us -> 43.7 us
  waiting for transfers between devices: 28.1 us -> 1.48 us
  starting transfers between devices: 21.3 us -> 3.87 us
  Pallas kernels: 27.4 us -> 25.9 us
    all_to_all x0 -> x2, blocking collectives: none -> 43.7 us  [the longest x1 24.3 us: shards(): lax.all_to_all(copies, ('zh', 'space'), 0, 0, tiled=True).reshape(-1, 2 * M)]
    all_to_all x2 -> x0, waiting for transfers between devices: 25.7 us -> none  [the longest x1 16.4 us: shards(): lax.all_to_all(sent, ('zh', 'space'), 0, 0, tiled=True).reshape(-1, 2 * M)]
    all_to_all x2 -> x0, starting transfers between devices: 17.4 us -> none  [the longest x1 9.36 us: shards(): lax.all_to_all(part.reshape(peers, 1, length), 'space', 0, 0, tiled=True)]
    pallas_call x1 -> x0, Pallas kernels: 1.11 us -> none  [spread(): pl.pallas_call(lambda *refs: spread_kernel(peers, copies, *refs), name='s...]
    ppermute x1, waiting for transfers between devices: 2.38 us -> 1.48 us  [shards(): other = lax.ppermute(mine, 'core', ((0, 1), (1, 0)))]
  transfers between devices with their start and end apart: 3 -> 1, of which waited for: 3 -> 1; matrix products, arithmetic and copies ran while one was open for 0% -> 0% of each run, Pallas kernels for 1% -> 1%
where the time goes in v3:
time: 77 us; the launch traced here: 76.7 us
  blocking collectives  43.7 us (57%)
  Pallas kernels  25.9 us (34%)
  starting transfers between devices  3.87 us (5%)
  waiting for transfers between devices  1.48 us (2%)
  between operations  0.86 us (1%)
    all_to_all x1, blocking collectives, shards(): lax.all_to_all(copies, ('zh', 'space'), 0, 0, tiled=True).reshape(-1, 2 * M)  24.3 us
    all_to_all x1, blocking collectives, shards(): lax.all_to_all(part.reshape(peers, 1, length), 'space', 0, 0, tiled=True)  19.4 us
    pallas_call x1, Pallas kernels, solve(): pl.pallas_call(lambda *refs: solve_kernel(points, peers, *refs), name='so...  14.7 us
    pallas_call x1, Pallas kernels, project(): pl.pallas_call(lambda *refs: project_kernel(points, peers, *refs), name='...  10.3 us
    ppermute x1, starting transfers between devices, shards(): other = lax.ppermute(mine, 'core', ((0, 1), (1, 0)))  3.87 us
  transfers between devices with their start and end apart: 1, of which 1 were waited for; matrix products, arithmetic and copies ran while one was open for 0% of the time, Pallas kernels for 1%

profile of v3, /device:TPU:1, one launch (start us, length us, event | category | flops | bytes accessed | tf_op | source)
XLA Modules:
  0.0 76.7 jit_solution(14858744943922462132)
XLA Ops:
  0.6 10.3 %project.1.refs_2_ = f32[1088,128]{1,0:T(8,128)} custom-call(s32[8]{0:T(128)} %refs_0_.3, bf16[2,1024,4096]{2,1,0:T(8,128)(2,1)} %refs_1_.2, bf16[2,64,4096]{2,1,0:T(8,128)(2,1)} %refs_1_.3), custom_call_target="tpu_custom_call" | custom-call | tf_op jit(solution)/shard_map/project/pallas_call | solution.py:67
  10.9 19.4 %all_to_all.10 = f32[32,1,4352]{2,1,0:T(1,128)S(1)} all-to-all(f32[32,1,4352]{2,1,0:T(1,128)} %bitcast.2), channel_id=1, replica_groups=mesh['zh'=2,'core'=2,'space'=32] {'space'}, dimensions={0} | all-to-all | bytes 1114112 | tf_op jit(solution)/shard_map/all_to_all | solution.py:352
  30.3 0.3 reduce_sum.11
  30.6 0.6 broadcast_in_dim.3
  31.2 0.0 copy-start
  31.2 0.0 copy-start.1
  31.2 0.0 copy-start.3
  31.3 24.3 %all_to_all.11 = f32[64,1,4352]{2,1,0:T(1,128)S(1)} all-to-all(f32[64,1,4352]{2,1,0:T(1,128)S(1)} %broadcast_in_dim.3), channel_id=1, replica_groups=mesh['zh'=2,'core'=2,'space'=32] {'zh','space'}, dimensions={0} | all-to-all | bytes 2228224 | tf_op jit(solution)/shard_map/all_to_all | solution.py:356
  55.6 0.0 copy-start.2
  55.6 3.9 %collective-permute-start = (f32[2176,128]{1,0:T(8,128)S(1)}, f32[2176,128]{1,0:T(8,128)S(1)}, u32[]{:S(2)}, u32[]{:S(2)}) collective-permute-start(f32[2176,128]{1,0:T(8,128)S(1)} %bitcast.3), channel_id=1, source_target_pairs={{0,32},{32,0},{1,33},{33,1},{2,34},{34,2},{3,35},{35,3},{4,36},{36... | collective-permute-start | bytes 3342344 | tf_op jit(solution)/shard_map/ppermute | solution.py:358
  59.5 0.0 copy-done
  59.5 0.0 copy-done.1
  59.5 0.0 copy-done.3
  59.5 0.8 %mask.1.refs_3_ = bf16[2,64,4096]{2,1,0:T(8,128)(2,1)S(1)} custom-call(s32[8]{0:T(128)S(1)} %copy-done.3, bf16[2,64,4096]{2,1,0:T(8,128)(2,1)S(1)} %copy-done.1, f32[1088,128]{1,0:T(8,128)S(1)} %copy-done), custom_call_target="tpu_custom_call" | custom-call | flops 524288 | bytes 2097152 | tf_op jit(solution)/shard_map/mask/pallas_call | solution.py:315
  60.3 0.0 copy-done.2
  60.3 0.1 pair.1.refs_2_
  60.4 1.5 %collective-permute-done.refs_1_ = f32[2176,128]{1,0:T(8,128)S(1)} collective-permute-done((f32[2176,128]{1,0:T(8,128)S(1)}, f32[2176,128]{1,0:T(8,128)S(1)}, u32[]{:S(2)}, u32[]{:S(2)}) %collective-permute-start) | collective-permute-done | bytes 1114144 | tf_op jit(solution)/shard_map/ppermute | solution.py:358
  61.9 14.7 %solve.1 = (bf16[2,128,4096]{2,1,0:T(8,128)(2,1)}, f32[1024,128]{1,0:T(8,128)}, f32[2,1024]{1,0:T(2,128)}) custom-call(f32[2176,128]{1,0:T(8,128)S(1)} %bitcast.4, f32[2176,128]{1,0:T(8,128)S(1)} %collective-permute-done.refs_1_, bf16[512,256]{1,0:T(8,128)(2,1)S(1)} %pair.1.refs_2_, bf16[2,64,4096]{2,1,0:T(8,128)(2,1)S(1)} %mask.1.refs_3_), custom_call_target="tpu_custom_call" | custom-call | tf_op jit(solution)/shard_map/solve/pallas_call | solution.py:279
  (1 shorter events, 0.0 us)
Async XLA Ops:
  31.2 28.3 %copy-start = (f32[1088,128]{1,0:T(8,128)S(1)}, f32[1088,128]{1,0:T(8,128)}, u32[]{:S(2)}) copy-start(f32[1088,128]{1,0:T(8,128)} %project.1.refs_2_) | copy-start | bytes 1671172
  31.2 28.2 %copy-start.1 = (bf16[2,64,4096]{2,1,0:T(8,128)(2,1)S(1)}, bf16[2,64,4096]{2,1,0:T(8,128)(2,1)}, u32[]{:S(2)}) copy-start(bf16[2,64,4096]{2,1,0:T(8,128)(2,1)} %refs_1_.3) | copy-start | bytes 3145732
  31.2 28.2 %copy-start.3 = (s32[8]{0:T(128)S(1)}, s32[8]{0:T(128)}, u32[]{:S(2)}) copy-start(s32[8]{0:T(128)} %refs_0_.3) | copy-start | bytes 100
  55.6 4.7 %copy-start.2 = (f32[512,128]{1,0:T(8,128)S(1)}, f32[512,128]{1,0:T(8,128)}, u32[]{:S(2)}) copy-start(f32[512,128]{1,0:T(8,128)} %x_ref.1) | copy-start | bytes 786436
  55.6 6.2 %collective-permute-start = (f32[2176,128]{1,0:T(8,128)S(1)}, f32[2176,128]{1,0:T(8,128)S(1)}, u32[]{:S(2)}, u32[]{:S(2)}) collective-permute-start(f32[2176,128]{1,0:T(8,128)S(1)} %bitcast.3), channel_id=1, source_target_pairs={{0,32},{32,0},{1,33},{33,1},{2,34},{34,2},{3,35},{35,3},{4,36},{36... | collective-permute-start | bytes 3342344 | tf_op jit(solution)/shard_map/ppermute | solution.py:358

commit v4 on v3

--- a/solution.py
+++ b/solution.py
@@ -105,8 +105,8 @@
     return jnp.concatenate(halves(x), axis=1)
 
 
-def product(left, pair):
-    return folded(dot(left, jnp.concatenate([pair, pair], axis=0), 1, 0))
+def product(high, middle, pair):
+    return folded(dot(high, pair, 1, 0)) + dot(middle, pair[:, :K], 1, 0)
 
 
 def gram_of(image):
@@ -216,7 +216,7 @@
     cov_ref[:, :joint], cov_ref[:, joint:] = halves(cov)
     basis_pair = start_ref[...]
     for _ in range(SWEEPS):
-        image = product(cov_ref[...], basis_pair)
+        image = product(cov_ref[:, :joint], cov_ref[:, joint:], basis_pair)
         factor = inverse_factor(gram_of(image), left_ref, made_ref, factor_ref)
         basis = times_transposed(image, factor)
         basis_pair = pair_up(basis)
@@ -232,7 +232,7 @@
         copy = pltpu.make_async_copy(out_ref.at[part], load_ref.at[part], sem.at[at // STEP])
         copy.start()
         copies.append(copy)
-    scores = product(jnp.concatenate([high_ref[...], middle_ref[...]], axis=1), basis_pair)
+    scores = product(high_ref[...], middle_ref[...], basis_pair)
     score_out_ref[...] = scores
     copy = pltpu.make_async_copy(score_out_ref, score_ref, score_sem)
     copy.start()

time: 77 us -> 76.1 us (0.988)
  Pallas kernels: 25.9 us -> 24.9 us
    pallas_call x1, Pallas kernels: 14.7 us -> 13.8 us  [solve(): pl.pallas_call(lambda *refs: solve_kernel(points, peers, *refs), name='so...]
where the time goes in v4:
time: 76.1 us; the launch traced here: 75.8 us
  blocking collectives  43.7 us (57%)
  Pallas kernels  24.9 us (33%)
  starting transfers between devices  3.87 us (5%)
  waiting for transfers between devices  1.48 us (2%)
  between operations  0.86 us (1%)
    all_to_all x1, blocking collectives, shards(): lax.all_to_all(copies, ('zh', 'space'), 0, 0, tiled=True).reshape(-1, 2 * M)  24.3 us
    all_to_all x1, blocking collectives, shards(): lax.all_to_all(part.reshape(peers, 1, length), 'space', 0, 0, tiled=True)  19.4 us
    pallas_call x1, Pallas kernels, solve(): pl.pallas_call(lambda *refs: solve_kernel(points, peers, *refs), name='so...  13.8 us
    pallas_call x1, Pallas kernels, project(): pl.pallas_call(lambda *refs: project_kernel(points, peers, *refs), name='...  10.3 us
    ppermute x1, starting transfers between devices, shards(): other = lax.ppermute(mine, 'core', ((0, 1), (1, 0)))  3.87 us
  transfers between devices with their start and end apart: 1, of which 1 were waited for; matrix products, arithmetic and copies ran while one was open for 0% of the time, Pallas kernels for 1%

profile of v4, /device:TPU:1, one launch (start us, length us, event | category | flops | bytes accessed | tf_op | source)
XLA Modules:
  0.0 75.8 jit_solution(11468794674087581538)
XLA Ops:
  0.6 10.3 %project.1.refs_2_ = f32[1088,128]{1,0:T(8,128)} custom-call(s32[8]{0:T(128)} %refs_0_.3, bf16[2,1024,4096]{2,1,0:T(8,128)(2,1)} %refs_1_.2, bf16[2,64,4096]{2,1,0:T(8,128)(2,1)} %refs_1_.3), custom_call_target="tpu_custom_call" | custom-call | tf_op jit(solution)/shard_map/project/pallas_call | solution.py:67
  10.9 19.4 %all_to_all.10 = f32[32,1,4352]{2,1,0:T(1,128)S(1)} all-to-all(f32[32,1,4352]{2,1,0:T(1,128)} %bitcast.2), channel_id=1, replica_groups=mesh['zh'=2,'core'=2,'space'=32] {'space'}, dimensions={0} | all-to-all | bytes 1114112 | tf_op jit(solution)/shard_map/all_to_all | solution.py:352
  30.3 0.3 reduce_sum.11
  30.6 0.6 broadcast_in_dim.3
  31.2 0.0 copy-start
  31.2 0.0 copy-start.1
  31.2 0.0 copy-start.3
  31.3 24.3 %all_to_all.11 = f32[64,1,4352]{2,1,0:T(1,128)S(1)} all-to-all(f32[64,1,4352]{2,1,0:T(1,128)S(1)} %broadcast_in_dim.3), channel_id=1, replica_groups=mesh['zh'=2,'core'=2,'space'=32] {'zh','space'}, dimensions={0} | all-to-all | bytes 2228224 | tf_op jit(solution)/shard_map/all_to_all | solution.py:356
  55.6 0.0 copy-start.2
  55.6 3.9 %collective-permute-start = (f32[2176,128]{1,0:T(8,128)S(1)}, f32[2176,128]{1,0:T(8,128)S(1)}, u32[]{:S(2)}, u32[]{:S(2)}) collective-permute-start(f32[2176,128]{1,0:T(8,128)S(1)} %bitcast.3), channel_id=1, source_target_pairs={{0,32},{32,0},{1,33},{33,1},{2,34},{34,2},{3,35},{35,3},{4,36},{36... | collective-permute-start | bytes 3342344 | tf_op jit(solution)/shard_map/ppermute | solution.py:358
  59.5 0.0 copy-done
  59.5 0.0 copy-done.1
  59.5 0.0 copy-done.3
  59.5 0.8 %mask.1.refs_3_ = bf16[2,64,4096]{2,1,0:T(8,128)(2,1)S(1)} custom-call(s32[8]{0:T(128)S(1)} %copy-done.3, bf16[2,64,4096]{2,1,0:T(8,128)(2,1)S(1)} %copy-done.1, f32[1088,128]{1,0:T(8,128)S(1)} %copy-done), custom_call_target="tpu_custom_call" | custom-call | flops 524288 | bytes 2097152 | tf_op jit(solution)/shard_map/mask/pallas_call | solution.py:315
  60.3 0.0 copy-done.2
  60.3 0.1 pair.1.refs_2_
  60.4 1.5 %collective-permute-done.refs_1_ = f32[2176,128]{1,0:T(8,128)S(1)} collective-permute-done((f32[2176,128]{1,0:T(8,128)S(1)}, f32[2176,128]{1,0:T(8,128)S(1)}, u32[]{:S(2)}, u32[]{:S(2)}) %collective-permute-start) | collective-permute-done | bytes 1114144 | tf_op jit(solution)/shard_map/ppermute | solution.py:358
  61.9 13.8 %solve.1 = (bf16[2,128,4096]{2,1,0:T(8,128)(2,1)}, f32[1024,128]{1,0:T(8,128)}, f32[2,1024]{1,0:T(2,128)}) custom-call(f32[2176,128]{1,0:T(8,128)S(1)} %bitcast.4, f32[2176,128]{1,0:T(8,128)S(1)} %collective-permute-done.refs_1_, bf16[512,256]{1,0:T(8,128)(2,1)S(1)} %pair.1.refs_2_, bf16[2,64,4096]{2,1,0:T(8,128)(2,1)S(1)} %mask.1.refs_3_), custom_call_target="tpu_custom_call" | custom-call | tf_op jit(solution)/shard_map/solve/pallas_call | solution.py:279
  (1 shorter events, 0.0 us)
Async XLA Ops:
  31.2 28.3 %copy-start = (f32[1088,128]{1,0:T(8,128)S(1)}, f32[1088,128]{1,0:T(8,128)}, u32[]{:S(2)}) copy-start(f32[1088,128]{1,0:T(8,128)} %project.1.refs_2_) | copy-start | bytes 1671172
  31.2 28.2 %copy-start.1 = (bf16[2,64,4096]{2,1,0:T(8,128)(2,1)S(1)}, bf16[2,64,4096]{2,1,0:T(8,128)(2,1)}, u32[]{:S(2)}) copy-start(bf16[2,64,4096]{2,1,0:T(8,128)(2,1)} %refs_1_.3) | copy-start | bytes 3145732
  31.2 28.2 %copy-start.3 = (s32[8]{0:T(128)S(1)}, s32[8]{0:T(128)}, u32[]{:S(2)}) copy-start(s32[8]{0:T(128)} %refs_0_.3) | copy-start | bytes 100
  55.6 4.7 %copy-start.2 = (f32[512,128]{1,0:T(8,128)S(1)}, f32[512,128]{1,0:T(8,128)}, u32[]{:S(2)}) copy-start(f32[512,128]{1,0:T(8,128)} %x_ref.1) | copy-start | bytes 786436
  55.6 6.2 %collective-permute-start = (f32[2176,128]{1,0:T(8,128)S(1)}, f32[2176,128]{1,0:T(8,128)S(1)}, u32[]{:S(2)}, u32[]{:S(2)}) collective-permute-start(f32[2176,128]{1,0:T(8,128)S(1)} %bitcast.3), channel_id=1, source_target_pairs={{0,32},{32,0},{1,33},{33,1},{2,34},{34,2},{3,35},{35,3},{4,36},{36... | collective-permute-start | bytes 3342344 | tf_op jit(solution)/shard_map/ppermute | solution.py:358

commit v5 on v4

--- a/solution.py
+++ b/solution.py
@@ -111,11 +111,8 @@
 
 def gram_of(image):
     high, middle, low = thirds(image)
-    pair = jnp.concatenate([high, middle], axis=1)
-    main = folded(
-        dot(jnp.concatenate([high, middle], axis=0), jnp.concatenate([pair, pair], axis=0), 0, 0)
-    )
-    last = dot(high, low, 0, 0)
+    main = dot(high, high, 0, 0) + dot(middle, middle, 0, 0)
+    last = folded(dot(high, jnp.concatenate([middle, low], axis=1), 0, 0))
     return main + (last + last.T)
 
 

time: 76.1 us -> 76.1 us (level)
  no operation moved by 1% of the time
where the time goes in v5:
time: 76.1 us; the launch traced here: 75.8 us
  blocking collectives  43.7 us (57%)
  Pallas kernels  24.9 us (33%)
  starting transfers between devices  3.87 us (5%)
  waiting for transfers between devices  1.48 us (2%)
  between operations  0.86 us (1%)
    all_to_all x1, blocking collectives, shards(): lax.all_to_all(copies, ('zh', 'space'), 0, 0, tiled=True).reshape(-1, 2 * M)  24.3 us
    all_to_all x1, blocking collectives, shards(): lax.all_to_all(part.reshape(peers, 1, length), 'space', 0, 0, tiled=True)  19.4 us
    pallas_call x1, Pallas kernels, solve(): pl.pallas_call(lambda *refs: solve_kernel(points, peers, *refs), name='so...  13.8 us
    pallas_call x1, Pallas kernels, project(): pl.pallas_call(lambda *refs: project_kernel(points, peers, *refs), name='...  10.3 us
    ppermute x1, starting transfers between devices, shards(): other = lax.ppermute(mine, 'core', ((0, 1), (1, 0)))  3.87 us
  transfers between devices with their start and end apart: 1, of which 1 were waited for; matrix products, arithmetic and copies ran while one was open for 0% of the time, Pallas kernels for 1%

profile of v5, /device:TPU:1, one launch (start us, length us, event | category | flops | bytes accessed | tf_op | source)
XLA Modules:
  0.0 75.8 jit_solution(4034050563182383095)
XLA Ops:
  0.6 10.3 %project.1.refs_2_ = f32[1088,128]{1,0:T(8,128)} custom-call(s32[8]{0:T(128)} %refs_0_.3, bf16[2,1024,4096]{2,1,0:T(8,128)(2,1)} %refs_1_.2, bf16[2,64,4096]{2,1,0:T(8,128)(2,1)} %refs_1_.3), custom_call_target="tpu_custom_call" | custom-call | tf_op jit(solution)/shard_map/project/pallas_call | solution.py:67
  10.9 19.4 %all_to_all.10 = f32[32,1,4352]{2,1,0:T(1,128)S(1)} all-to-all(f32[32,1,4352]{2,1,0:T(1,128)} %bitcast.2), channel_id=1, replica_groups=mesh['zh'=2,'core'=2,'space'=32] {'space'}, dimensions={0} | all-to-all | bytes 1114112 | tf_op jit(solution)/shard_map/all_to_all | solution.py:349
  30.3 0.3 reduce_sum.11
  30.6 0.6 broadcast_in_dim.3
  31.2 0.0 copy-start
  31.2 0.0 copy-start.1
  31.2 0.0 copy-start.3
  31.3 24.3 %all_to_all.11 = f32[64,1,4352]{2,1,0:T(1,128)S(1)} all-to-all(f32[64,1,4352]{2,1,0:T(1,128)S(1)} %broadcast_in_dim.3), channel_id=1, replica_groups=mesh['zh'=2,'core'=2,'space'=32] {'zh','space'}, dimensions={0} | all-to-all | bytes 2228224 | tf_op jit(solution)/shard_map/all_to_all | solution.py:353
  55.6 0.0 copy-start.2
  55.6 3.9 %collective-permute-start = (f32[2176,128]{1,0:T(8,128)S(1)}, f32[2176,128]{1,0:T(8,128)S(1)}, u32[]{:S(2)}, u32[]{:S(2)}) collective-permute-start(f32[2176,128]{1,0:T(8,128)S(1)} %bitcast.3), channel_id=1, source_target_pairs={{0,32},{32,0},{1,33},{33,1},{2,34},{34,2},{3,35},{35,3},{4,36},{36... | collective-permute-start | bytes 3342344 | tf_op jit(solution)/shard_map/ppermute | solution.py:355
  59.5 0.0 copy-done
  59.5 0.0 copy-done.1
  59.5 0.0 copy-done.3
  59.5 0.8 %mask.1.refs_3_ = bf16[2,64,4096]{2,1,0:T(8,128)(2,1)S(1)} custom-call(s32[8]{0:T(128)S(1)} %copy-done.3, bf16[2,64,4096]{2,1,0:T(8,128)(2,1)S(1)} %copy-done.1, f32[1088,128]{1,0:T(8,128)S(1)} %copy-done), custom_call_target="tpu_custom_call" | custom-call | flops 524288 | bytes 2097152 | tf_op jit(solution)/shard_map/mask/pallas_call | solution.py:312
  60.3 0.0 copy-done.2
  60.3 0.1 pair.1.refs_2_
  60.4 1.5 %collective-permute-done.refs_1_ = f32[2176,128]{1,0:T(8,128)S(1)} collective-permute-done((f32[2176,128]{1,0:T(8,128)S(1)}, f32[2176,128]{1,0:T(8,128)S(1)}, u32[]{:S(2)}, u32[]{:S(2)}) %collective-permute-start) | collective-permute-done | bytes 1114144 | tf_op jit(solution)/shard_map/ppermute | solution.py:355
  61.9 13.8 %solve.1 = (bf16[2,128,4096]{2,1,0:T(8,128)(2,1)}, f32[1024,128]{1,0:T(8,128)}, f32[2,1024]{1,0:T(2,128)}) custom-call(f32[2176,128]{1,0:T(8,128)S(1)} %bitcast.4, f32[2176,128]{1,0:T(8,128)S(1)} %collective-permute-done.refs_1_, bf16[512,256]{1,0:T(8,128)(2,1)S(1)} %pair.1.refs_2_, bf16[2,64,4096]{2,1,0:T(8,128)(2,1)S(1)} %mask.1.refs_3_), custom_call_target="tpu_custom_call" | custom-call | tf_op jit(solution)/shard_map/solve/pallas_call | solution.py:276
  (1 shorter events, 0.0 us)
Async XLA Ops:
  31.2 28.3 %copy-start = (f32[1088,128]{1,0:T(8,128)S(1)}, f32[1088,128]{1,0:T(8,128)}, u32[]{:S(2)}) copy-start(f32[1088,128]{1,0:T(8,128)} %project.1.refs_2_) | copy-start | bytes 1671172
  31.2 28.2 %copy-start.1 = (bf16[2,64,4096]{2,1,0:T(8,128)(2,1)S(1)}, bf16[2,64,4096]{2,1,0:T(8,128)(2,1)}, u32[]{:S(2)}) copy-start(bf16[2,64,4096]{2,1,0:T(8,128)(2,1)} %refs_1_.3) | copy-start | bytes 3145732
  31.2 28.2 %copy-start.3 = (s32[8]{0:T(128)S(1)}, s32[8]{0:T(128)}, u32[]{:S(2)}) copy-start(s32[8]{0:T(128)} %refs_0_.3) | copy-start | bytes 100
  55.6 4.7 %copy-start.2 = (f32[512,128]{1,0:T(8,128)S(1)}, f32[512,128]{1,0:T(8,128)}, u32[]{:S(2)}) copy-start(f32[512,128]{1,0:T(8,128)} %x_ref.1) | copy-start | bytes 786436
  55.6 6.2 %collective-permute-start = (f32[2176,128]{1,0:T(8,128)S(1)}, f32[2176,128]{1,0:T(8,128)S(1)}, u32[]{:S(2)}, u32[]{:S(2)}) collective-permute-start(f32[2176,128]{1,0:T(8,128)S(1)} %bitcast.3), channel_id=1, source_target_pairs={{0,32},{32,0},{1,33},{33,1},{2,34},{34,2},{3,35},{35,3},{4,36},{36... | collective-permute-start | bytes 3342344 | tf_op jit(solution)/shard_map/ppermute | solution.py:355
